TPU v7x, 256 devices: a whole 4x4x8 slice. The times are simulated.
256 devices in a mesh: rep: 32 (over y, z), tp: 8 (over x, core).
Axes of the slice: x: 4, y: 4, z: 8, core: 2. Of those that a mesh axis runs over, the one named last changes fastest.
Arguments:
- reference_rows: bfloat16 [32768, 8192], P('rep', 'tp'), may hold values from -7 to 7
- critic_rows: bfloat16 [32768, 4096], P('rep', 'tp'), may hold values from -7 to 7
- segment_ids: int32 [32768], P('rep'), may hold values from -1 to 32767, as said below
- pack_dest: int32 [32, 32], P('rep'), may hold values from 0 to 31, as said below
- ref_query: bfloat16 [8192, 4096], P('rep', 'tp'), may hold values from -2 to 2
- ref_key: bfloat16 [8192, 1024], P('rep', 'tp'), may hold values from -2 to 2
- ref_value: bfloat16 [8192, 1024], P('rep', 'tp'), may hold values from -0.0625 to 0.0625
- critic_query: bfloat16 [4096, 4096], P(None, 'tp'), may hold values from -2 to 2
- critic_key: bfloat16 [4096, 1024], P(None, 'tp'), may hold values from -2 to 2
- critic_value: bfloat16 [4096, 1024], P(None, 'tp'), may hold values from -0.09375 to 0.09375
- ref_readout: bfloat16 [4096], P('tp'), may hold values from -0.09375 to 0.09375
- critic_readout: bfloat16 [4096], P('tp'), may hold values from -0.09375 to 0.09375
Outputs:
- ref_score: float32 [32768], P('rep')
- value: float32 [32768], P('rep')
Inputs may be any that keep to these rules, and one draw needn't show every extreme that they name: Each row is a permutation: block b of replica s goes to pack pack_dest[s, b]. `segment_ids`: in every aligned block of 32 slots the used rows come first and the rest hold -1; a block holds 1 to 31 used rows, and every pack receives exactly 31 used rows from some replica and exactly 512 used rows in all. A rollout is a run of consecutive used rows with one id inside one block; different rollouts have different ids.
All inputs are finite; a program needn't handle non-finite values.
Results may differ from a plain program's by a relative error of at most 0.0084.
Values may be sent and summed in bfloat16 or wider, within the bound.
No kernel may reach another device: no remote copies, remote signals or barrier semaphores. Data moves between devices by JAX's collectives and lax.ppermute only.
A program may use at most 128 MiB of HBM per device.

v0:
```python
import jax
import jax.numpy as jnp
from jax import lax
from jax.sharding import PartitionSpec as P

HD = 128


def normalize(source):
    widened = source.astype(jnp.float32)
    scale_row = lax.rsqrt(jnp.mean(widened * widened, axis=-1, keepdims=True) + 1e-05)
    return (widened * scale_row).astype(jnp.bfloat16)


def attend(queries, keys_in, values_in, segments):
    row_count = queries.shape[0]
    groups = keys_in.shape[1] // HD
    shared = queries.shape[1] // keys_in.shape[1]
    query_four = queries.reshape(row_count, groups, shared, HD)
    key_three = keys_in.reshape(row_count, groups, HD)
    value_three = values_in.reshape(row_count, groups, HD)
    scores = jnp.einsum(
        "pgjd,qgd->gjpq", query_four, key_three, preferred_element_type=jnp.float32
    ) * HD ** (-0.5)
    position = jnp.arange(row_count)
    allowed = (position[None, :] <= position[:, None]) & (segments[:, None] == segments[None, :])
    masked = jnp.where(allowed, scores, -1e30)
    row_max = jnp.max(masked, axis=-1, keepdims=True)
    powers = jnp.where(allowed, jnp.exp(masked - row_max), 0.0)
    weights = (powers / jnp.sum(powers, axis=-1, keepdims=True)).astype(jnp.bfloat16)
    mixture = jnp.einsum("gjpq,qgd->pgjd", weights, value_three, preferred_element_type=jnp.float32)
    return mixture.reshape(row_count, groups * shared * HD).astype(jnp.bfloat16)


def compact_index(segments):
    row_count = segments.shape[0]
    sort_keys = jnp.where(segments >= 0, 0, row_count).astype(jnp.int32) + jnp.arange(
        row_count, dtype=jnp.int32
    )
    return jnp.argsort(sort_keys)[: row_count // 2]


def project(normed, weight):
    return jnp.dot(normed, weight, preferred_element_type=jnp.float32).astype(jnp.bfloat16)


def body(
    reference_rows,
    critic_rows,
    segment_ids,
    pack_dest,
    ref_query,
    ref_key,
    ref_value,
    critic_query,
    critic_key,
    critic_value,
    ref_readout,
    critic_readout,
):
    replicas = lax.axis_size("rep")
    slot_count = segment_ids.shape[0]
    block_rows = slot_count // replicas
    destination = pack_dest[0]
    inverse = jnp.argsort(destination)

    def by_pack(source):
        blocks = source.reshape((replicas, block_rows) + source.shape[1:])
        return jnp.take(blocks, inverse, axis=0).reshape(source.shape)

    ref_in, critic_in, ids_in = (
        lax.all_to_all(by_pack(reference_rows), "rep", split_axis=0, concat_axis=0, tiled=True),
        lax.all_to_all(by_pack(critic_rows), "rep", split_axis=0, concat_axis=0, tiled=True),
        lax.all_to_all(by_pack(segment_ids), "rep", split_axis=0, concat_axis=0, tiled=True),
    )
    chosen = compact_index(ids_in)
    pack_ids = ids_in[chosen]
    ref_full, critic_full = (
        lax.all_gather(ref_in[chosen], "tp", axis=1, tiled=True),
        lax.all_gather(critic_in[chosen], "tp", axis=1, tiled=True),
    )
    critic_normed = normalize(critic_full)
    critic_attn = attend(
        project(critic_normed, critic_query),
        project(critic_normed, critic_key),
        project(critic_normed, critic_value),
        pack_ids,
    )
    ref_normed = normalize(ref_full)
    pieces = (
        lax.all_gather(ref_query, "rep", axis=0, tiled=True),
        lax.all_gather(ref_key, "rep", axis=0, tiled=True),
        lax.all_gather(ref_value, "rep", axis=0, tiled=True),
    )
    ref_q, ref_k, ref_v = tuple(
        (
            jnp.dot(ref_normed, weight_piece, preferred_element_type=jnp.float32)
            for weight_piece in pieces
        )
    )
    ref_attn = attend(
        ref_q.astype(jnp.bfloat16), ref_k.astype(jnp.bfloat16), ref_v.astype(jnp.bfloat16), pack_ids
    )
    ref_spread = jnp.zeros((slot_count, ref_attn.shape[1]), jnp.bfloat16).at[chosen].set(ref_attn)
    critic_spread = (
        jnp.zeros((slot_count, critic_attn.shape[1]), jnp.bfloat16).at[chosen].set(critic_attn)
    )
    ref_home, critic_home = (
        lax.all_to_all(ref_spread, "rep", split_axis=0, concat_axis=0, tiled=True),
        lax.all_to_all(critic_spread, "rep", split_axis=0, concat_axis=0, tiled=True),
    )
    ref_home = jnp.take(ref_home.reshape(replicas, block_rows, -1), destination, axis=0).reshape(
        slot_count, -1
    )
    critic_home = jnp.take(
        critic_home.reshape(replicas, block_rows, -1), destination, axis=0
    ).reshape(slot_count, -1)
    partial_value = jnp.stack(
        [
            jnp.dot(ref_home, ref_readout, preferred_element_type=jnp.float32),
            jnp.dot(critic_home, critic_readout, preferred_element_type=jnp.float32),
        ]
    )
    ordered = lax.psum(partial_value, "tp")
    ordered = jnp.where(segment_ids[None, :] >= 0, ordered, 0.0)
    return (ordered[0], ordered[1])


def solution(mesh):
    return jax.shard_map(
        body,
        mesh=mesh,
        in_specs=(
            P("rep", "tp"),
            P("rep", "tp"),
            P("rep"),
            P("rep", None),
            P("rep", "tp"),
            P("rep", "tp"),
            P("rep", "tp"),
            P(None, "tp"),
            P(None, "tp"),
            P(None, "tp"),
            P("tp"),
            P("tp"),
        ),
        out_specs=(P("rep"), P("rep")),
        check_vma=False,
    )
```

profile of v0, /device:TPU:1, one launch (start us, length us, event | category | flops | bytes accessed | tf_op | source)
XLA Modules:
  0.0 513.6 jit_solution(6631517655676095522)
XLA Ops:
  11.6 12.0 %all-to-all-start = ((s32[32,32,1]{1,2,0:T(1,128)}), s32[32,32,1]{1,2,0:T(1,128)S(1)}, u32[]{:S(2)}, u32[]{:S(2)}) async-start(s32[32,32,1]{1,2,0:T(1,128)} %bitcast.2), calls=%async_computation | async-start | bytes 32768 | tf_op jit(solution)/shard_map/all_to_all | solution.py:74
  26.7 5.6 %all-to-all-done = s32[32,32,1]{1,2,0:T(1,128)S(1)} async-done(((s32[32,32,1]{1,2,0:T(1,128)}), s32[32,32,1]{1,2,0:T(1,128)S(1)}, u32[]{:S(2)}, u32[]{:S(2)}) %all-to-all-start) | async-done | bytes 4128 | tf_op jit(solution)/shard_map/all_to_all | solution.py:74
  32.3 3.9 all-to-all-start.3
  37.6 4.4 sort.35
  41.9 18.7 %all-to-all-done.3 = bf16[32,32,512]{2,1,0:T(8,128)(2,1)S(1)} async-done(((bf16[32,32,512]{2,1,0:T(8,128)(2,1)}), bf16[32,32,512]{2,1,0:T(8,128)(2,1)S(1)}, u32[]{:S(2)}, u32[]{:S(2)}) %all-to-all-start.3) | async-done | bytes 1048608 | tf_op jit(solution)/shard_map/all_to_all | solution.py:73
  67.2 55.1 %all_to_all.45 = bf16[32,32,1024]{2,1,0:T(8,128)(2,1)} all-to-all(bf16[32,32,1024]{2,1,0:T(8,128)(2,1)S(1)} %broadcast_select_fusion), channel_id=1, replica_groups=mesh['rep'=32,'tp'=8] {'rep'}, dimensions={0} | all-to-all | bytes 4194304 | tf_op jit(solution)/shard_map/all_to_all | solution.py:72
  122.3 5.4 %gather_fusion.2 = bf16[512,1024]{1,0:T(8,128)(2,1)} fusion(bf16[1024,1024]{1,0:T(8,128)(2,1)} %bitcast.109, s32[1024]{0:T(1024)S(1)} %pad_clamp_fusion.1), kind=kCustom, calls=%fused_computation.5 | custom fusion | bytes 2099200 | tf_op jit(solution)/shard_map/gather | solution.py:79
  136.0 4.7 convolution_convert_fusion
  140.8 40.8 %all-gather.14.cloned.1.call-done = bf16[512,8192]{1,0:T(8,128)(2,1)} async-done(((bf16[512,1024]{1,0:T(8,128)(2,1)}), bf16[512,8192]{1,0:T(8,128)(2,1)}) %all-gather.14.cloned.1.call-update) | async-done | bytes 8388624 | tf_op jit(solution)/shard_map/all_gather | solution.py:79
  181.5 5.1 fusion
  186.6 95.4 %all-gather.12.cloned.1.call-done = bf16[8192,512]{1,0:T(8,128)(2,1)} async-done(((bf16[256,512]{1,0:T(8,128)(2,1)}), bf16[8192,512]{1,0:T(8,128)(2,1)}) %all-gather.12.cloned.1.call-update) | async-done | bytes 8388624 | tf_op jit(solution)/shard_map/all_gather | solution.py:91
  282.1 11.2 %convolution_convert_fusion.1 = bf16[512,512]{0,1:T(8,128)(2,1)} fusion(bf16[8192,512]{1,0:T(8,128)(2,1)} %all-gather.12.cloned.1.call-done, bf16[512,8192]{1,0:T(8,128)(2,1)} %all-gather.14.cloned.1.call-done, f32[512]{0:T(512)S(1)} %add_rsqrt_fusion.1), kind=kOutput, calls=%fused_computation.38 | convolution fusion | flops 4307812352 | bytes 17303552 | tf_op jit(solution)/shard_map/dot_general | solution.py:97
  293.3 62.8 %all-gather.10.cloned.1.call-done = bf16[8192,128]{1,0:T(8,128)(2,1)} async-done(((bf16[256,128]{1,0:T(8,128)(2,1)}), bf16[8192,128]{1,0:T(8,128)(2,1)}) %all-gather.10.cloned.1.call-update) | async-done | bytes 2097168 | tf_op jit(solution)/shard_map/all_gather | solution.py:92
  356.1 10.2 %fusion.4 = (f32[4,512]{1,0:T(4,128)S(1)}, f32[512,512,4]{1,0,2:T(8,128)}) fusion(pred[512,512]{0,1:T(8,128)(4,1)S(1)} %fusion.26, bf16[512,4,128]{0,2,1:T(8,128)(2,1)} %bitcast.122, bf16[8192,128]{1,0:T(8,128)(2,1)} %all-gather.10.cloned.1.call-done, bf16[512,8192]{1,0:T(8,128)(2,1)} %all-gather.14.cloned.1.call-done, f32[512]{0:T(512)S(1)} %add_rsqrt_fusion.1), kind=kOutput, calls=%fused_computation.24 | convolution fusion | flops 1357969408 | bytes 15476736 | tf_op jit(solution)/shard_map/pgjd,qgd->gjpq/dot_general | solution.py:22
  366.3 9.5 %fusion.6 = (f32[4,512]{1,0:T(4,128)S(1)}, f32[4,512]{1,0:T(4,128)S(1)}, f32[512,512,4]{1,0,2:T(8,128)}) fusion(f32[512,512,4]{1,0,2:T(8,128)} %get-tuple-element.14, f32[4,512]{1,0:T(4,128)S(1)} %get-tuple-element.13, pred[512,512]{0,1:T(8,128)(4,1)S(1)} %fusion.26, bf16[512,4,128]{0,2,1:T(8,128)(2,1)S(1)} %bitcast.121, bf16[4096,128]{1,0:T(8,128)(2,1)} %param.22, ...), kind=kOutput, calls=%fused_computation.26 | convolution fusion | flops 820047872 | bytes 14444544 | tf_op jit(solution)/shard_map/pgjd,qgd->gjpq/dot_general | solution.py:22
  379.0 6.6 %fusion.17 = bf16[128,4,512]{2,0,1:T(8,128)(2,1)S(1)} fusion(f32[4,512]{1,0:T(4,128)S(1)} %fusion.7, f32[4,512]{1,0:T(4,128)S(1)} %get-tuple-element.8, f32[512,512,4]{1,0,2:T(8,128)} %get-tuple-element.15, pred[512,512]{0,1:T(8,128)(4,1)S(1)} %fusion.26, bf16[4096,128]{1,0:T(8,128)(2,1)} %param.23, bf16[512,4096]{1,0:T(8,128)(2,1)} %all-gather.16.cloned.1.call-done, ...), kind=kOutput, calls=%fused_computation.37 | convolution fusion | flops 818216960 | bytes 10242048 | tf_op jit(solution)/shard_map/gjpq,qgd->pgjd/dot_general | solution.py:31
  385.8 3.5 scatter_custom_fusion.1
  389.4 5.3 %all-to-all-start.4 = ((bf16[32,32,512]{2,1,0:T(8,128)(2,1)}), bf16[32,32,512]{2,1,0:T(8,128)(2,1)S(1)}, u32[]{:S(2)}, u32[]{:S(2)}) async-start(bf16[32,32,512]{2,1,0:T(8,128)(2,1)} %bitcast.113), calls=%async_computation.4 | async-start | bytes 2097152 | tf_op jit(solution)/shard_map/all_to_all | solution.py:110
  394.7 42.2 %all-gather.8.cloned.1.call-done = bf16[8192,128]{1,0:T(8,128)(2,1)} async-done(((bf16[256,128]{1,0:T(8,128)(2,1)}), bf16[8192,128]{1,0:T(8,128)(2,1)}) %all-gather.8.cloned.1.call-update) | async-done | bytes 2097168 | tf_op jit(solution)/shard_map/all_gather | solution.py:93
  436.9 9.9 %fusion.14 = bf16[128,4,512]{2,0,1:T(8,128)(2,1)} fusion(f32[4,512]{1,0:T(4,128)S(1)} %get-tuple-element.7, f32[4,512]{1,0:T(4,128)S(1)} %get-tuple-element.13, f32[512,512,4]{1,0,2:T(8,128)} %get-tuple-element.14, pred[512,512]{0,1:T(8,128)(4,1)S(1)} %fusion.26, bf16[8192,128]{1,0:T(8,128)(2,1)} %all-gather.8.cloned.1.call-done, ...), kind=kOutput, calls=%fused_computation.36 | convolution fusion | flops 1361379328 | bytes 15484928 | tf_op jit(solution)/shard_map/gjpq,qgd->pgjd/dot_general | solution.py:31
  448.9 4.0 scatter_custom_fusion
  452.9 6.5 %all-to-all-start.2 = ((bf16[32,32,512]{2,1,0:T(8,128)(2,1)}), bf16[32,32,512]{2,1,0:T(8,128)(2,1)}, u32[]{:S(2)}, u32[]{:S(2)}) async-start(bf16[32,32,512]{2,1,0:T(8,128)(2,1)} %bitcast.114), calls=%async_computation.2 | async-start | bytes 2097152 | tf_op jit(solution)/shard_map/all_to_all | solution.py:109
  461.3 19.5 %all-to-all-done.2 = bf16[32,32,512]{2,1,0:T(8,128)(2,1)} async-done(((bf16[32,32,512]{2,1,0:T(8,128)(2,1)}), bf16[32,32,512]{2,1,0:T(8,128)(2,1)}, u32[]{:S(2)}, u32[]{:S(2)}) %all-to-all-start.2) | async-done | bytes 1048608 | tf_op jit(solution)/shard_map/all_to_all | solution.py:109
  485.9 20.3 %psum.7 = f32[2,1024]{1,0:T(2,128)S(1)} all-reduce(f32[2,1024]{1,0:T(2,128)S(1)} %pad_maximum_fusion), channel_id=1, replica_groups=mesh['rep'=32,'tp'=8] {'tp'}, use_global_device_ids=true, to_apply=%region_10.12 | all-reduce | flops 2048 | bytes 16384 | tf_op jit(solution)/shard_map/psum | solution.py:124
  (68 shorter events, 36.8 us)
Async XLA Ops:
  7.2 56.2 %copy-start = (bf16[1024,1024]{1,0:T(8,128)(2,1)S(1)}, bf16[1024,1024]{1,0:T(8,128)(2,1)}, u32[]{:S(2)}) copy-start(bf16[1024,1024]{1,0:T(8,128)(2,1)} %param.14) | copy-start | bytes 6291460
  11.6 20.7 %all-to-all-start = ((s32[32,32,1]{1,2,0:T(1,128)}), s32[32,32,1]{1,2,0:T(1,128)S(1)}, u32[]{:S(2)}, u32[]{:S(2)}) async-start(s32[32,32,1]{1,2,0:T(1,128)} %bitcast.2), calls=%async_computation | async-start | bytes 32768 | tf_op jit(solution)/shard_map/all_to_all | solution.py:74
  32.3 28.3 %all-to-all-start.3 = ((bf16[32,32,512]{2,1,0:T(8,128)(2,1)}), bf16[32,32,512]{2,1,0:T(8,128)(2,1)S(1)}, u32[]{:S(2)}, u32[]{:S(2)}) async-start(bf16[32,32,512]{2,1,0:T(8,128)(2,1)} %broadcast_select_fusion.1), calls=%async_computation.3 | async-start | bytes 2097152 | tf_op jit(solution)/shard_map/all_to_all | solution.py:73
  36.2 96.4 %all-gather.16.cloned.1.call-start = ((), (), s32[]{:S(2)}) async-start(), calls=%async_computation.9 | async-start | bytes 4718592 | tf_op jit(solution)/shard_map/all_gather | solution.py:80
  63.3 118.3 %all-gather.14.cloned.1.call-start = ((), (), s32[]{:S(2)}) async-start(), calls=%async_computation.8 | async-start | bytes 9437184 | tf_op jit(solution)/shard_map/all_gather | solution.py:79
  127.7 154.4 %all-gather.12.cloned.1.call-start = ((), (), s32[]{:S(2)}) async-start(), calls=%async_computation.7 | async-start | bytes 8650752 | tf_op jit(solution)/shard_map/all_gather | solution.py:91
  128.4 227.6 %all-gather.10.cloned.1.call-start = ((), (), s32[]{:S(2)}) async-start(), calls=%async_computation.6 | async-start | bytes 2162688 | tf_op jit(solution)/shard_map/all_gather | solution.py:92
  129.0 307.9 %all-gather.8.cloned.1.call-start = ((), (), s32[]{:S(2)}) async-start(), calls=%async_computation.5 | async-start | bytes 2162688 | tf_op jit(solution)/shard_map/all_gather | solution.py:93
  132.6 3.5 copy-start.2
  389.4 63.5 %all-to-all-start.4 = ((bf16[32,32,512]{2,1,0:T(8,128)(2,1)}), bf16[32,32,512]{2,1,0:T(8,128)(2,1)S(1)}, u32[]{:S(2)}, u32[]{:S(2)}) async-start(bf16[32,32,512]{2,1,0:T(8,128)(2,1)} %bitcast.113), calls=%async_computation.4 | async-start | bytes 2097152 | tf_op jit(solution)/shard_map/all_to_all | solution.py:110
  446.8 12.6 %copy-start.4 = (bf16[512]{0:T(512)(128)(2,1)S(1)}, bf16[512]{0:T(512)(128)(2,1)}, u32[]{:S(2)}) copy-start(bf16[512]{0:T(512)(128)(2,1)} %param.24) | copy-start | bytes 3076
  446.8 12.6 %copy-start.5 = (bf16[512]{0:T(512)(128)(2,1)S(1)}, bf16[512]{0:T(512)(128)(2,1)}, u32[]{:S(2)}) copy-start(bf16[512]{0:T(512)(128)(2,1)} %param.25) | copy-start | bytes 3076
  446.8 12.6 %copy-start.6 = (s32[1,32]{1,0:T(1,128)S(1)}, s32[1,32]{1,0:T(1,128)}, u32[]{:S(2)}) copy-start(s32[1,32]{1,0:T(1,128)} %param.17) | copy-start | bytes 388
  446.8 12.7 %copy-start.3 = (s32[1024]{0:T(1024)S(1)}, s32[1024]{0:T(1024)}, u32[]{:S(2)}) copy-start(s32[1024]{0:T(1024)} %param.16) | copy-start | bytes 12292
  452.9 6.6 %copy-start.1 = (bf16[32,32,512]{2,1,0:T(8,128)(2,1)}, bf16[32,32,512]{2,1,0:T(8,128)(2,1)S(1)}, u32[]{:S(2)}) copy-start(bf16[32,32,512]{2,1,0:T(8,128)(2,1)S(1)} %all-to-all-done.4) | copy-start | bytes 3145732
  452.9 27.9 %all-to-all-start.2 = ((bf16[32,32,512]{2,1,0:T(8,128)(2,1)}), bf16[32,32,512]{2,1,0:T(8,128)(2,1)}, u32[]{:S(2)}, u32[]{:S(2)}) async-start(bf16[32,32,512]{2,1,0:T(8,128)(2,1)} %bitcast.114), calls=%async_computation.2 | async-start | bytes 2097152 | tf_op jit(solution)/shard_map/all_to_all | solution.py:109
Sparse Core Ops, SparseCore 0:
  63.4 36.1 all-gather.15
  127.8 53.6 all-gather.13
  184.1 97.8 all-gather.11
  284.5 71.5 all-gather.9
  358.5 78.3 all-gather.7
where the time goes:
time: 519 us; the launch traced here: 514 us
  waiting for transfers between devices  287 us (55%)
  blocking collectives  75.4 us (15%)
  matrix products  52.9 us (10%)
  local copies, waits for them, and re-layouts  31.9 us (6%)
  starting transfers between devices  27.9 us (5%)
  other arithmetic  24.5 us (5%)
  between operations  14.3 us (3%)
    all_gather x1, waiting for transfers between devices, body(): lax.all_gather(ref_query, 'rep', axis=0, tiled=True)  95.4 us
    all_gather x1, waiting for transfers between devices, body(): lax.all_gather(ref_key, 'rep', axis=0, tiled=True)  62.8 us
    all_to_all x1, blocking collectives, body(): lax.all_to_all(by_pack(reference_rows), 'rep', split_axis=0, concat_axis=...  55.1 us
    all_gather x1, waiting for transfers between devices, body(): lax.all_gather(ref_value, 'rep', axis=0, tiled=True)  42.2 us
    all_gather x1, waiting for transfers between devices, body(): lax.all_gather(ref_in[chosen], 'tp', axis=1, tiled=True)  40.8 us
    psum x1, blocking collectives, body(): ordered = lax.psum(partial_value, 'tp')  20.3 us
    dot_general x2, matrix products, attend(): jnp.einsum('pgjd,qgd->gjpq', query_four, key_three, preferred_element_typ...  19.7 us
    all_to_all x1, waiting for transfers between devices, body(): lax.all_to_all(ref_spread, 'rep', split_axis=0, concat_axis=0, tiled=True)  19.5 us
  transfers between devices with their start and end apart: 9, of which 7 were waited for; matrix products, arithmetic and copies ran while one was open for 19% of the time, Pallas kernels for 0%

commit v1 on v0

--- a/solution.py
+++ b/solution.py
@@ -4,6 +4,11 @@
 from jax.sharding import PartitionSpec as P
 
 HD = 128
+
+
+def exchange_gather(array, axis, d):
+    sent = jnp.stack([array] * lax.axis_size(axis))
+    return jnp.concatenate(lax.all_to_all(sent, axis, 0, 0), axis=d)
 
 
 def normalize(source):
@@ -90,7 +95,7 @@
     pieces = (
         lax.all_gather(ref_query, "rep", axis=0, tiled=True),
         lax.all_gather(ref_key, "rep", axis=0, tiled=True),
-        lax.all_gather(ref_value, "rep", axis=0, tiled=True),
+        exchange_gather(ref_value, "rep", 0),
     )
     ref_q, ref_k, ref_v = tuple(
         (

time: 519 us -> 481 us (0.927)
  waiting for transfers between devices: 287 us -> 238 us
  starting transfers between devices: 27.9 us -> 39 us
    all_gather x1 -> x0, waiting for transfers between devices: 42.2 us -> none  [body(): lax.all_gather(ref_value, 'rep', axis=0, tiled=True)]
    all_gather x1, waiting for transfers between devices: 40.8 us -> 30.6 us  [body(): lax.all_gather(ref_in[chosen], 'tp', axis=1, tiled=True)]
    all_to_all x0 -> x1, starting transfers between devices: none -> 8.16 us  [exchange_gather(): return jnp.concatenate(lax.all_to_all(sent, axis, 0, 0), axis=d)]
    all_to_all x1, waiting for transfers between devices: 0.01 us -> 6.38 us  [body(): lax.all_to_all(critic_spread, 'rep', split_axis=0, concat_axis=0, tiled=T...]
  transfers between devices with their start and end apart: 9 -> 9, of which waited for: 7 -> 7; matrix products, arithmetic and copies ran while one was open for 19% -> 20% of each run, Pallas kernels for 0% -> 0%
where the time goes in v1:
time: 481 us; the launch traced here: 475 us
  waiting for transfers between devices  238 us (49%)
  blocking collectives  76.3 us (16%)
  matrix products  52.1 us (11%)
  starting transfers between devices  39 us (8%)
  local copies, waits for them, and re-layouts  30.3 us (6%)
  other arithmetic  25.2 us (5%)
  between operations  14.3 us (3%)
    all_gather x1, waiting for transfers between devices, body(): lax.all_gather(ref_query, 'rep', axis=0, tiled=True)  95.4 us
    all_gather x1, waiting for transfers between devices, body(): lax.all_gather(ref_key, 'rep', axis=0, tiled=True)  62.8 us
    all_to_all x1, blocking collectives, body(): lax.all_to_all(by_pack(reference_rows), 'rep', split_axis=0, concat_axis=...  54.9 us
    all_gather x1, waiting for transfers between devices, body(): lax.all_gather(ref_in[chosen], 'tp', axis=1, tiled=True)  30.6 us
    psum x1, blocking collectives, body(): ordered = lax.psum(partial_value, 'tp')  21.4 us
    dot_general x2, matrix products, attend(): jnp.einsum('pgjd,qgd->gjpq', query_four, key_three, preferred_element_typ...  19.7 us
    all_to_all x1, waiting for transfers between devices, body(): lax.all_to_all(by_pack(critic_rows), 'rep', split_axis=0, concat_axis=0,...  18.7 us
    all_to_all x1, waiting for transfers between devices, body(): lax.all_to_all(ref_spread, 'rep', split_axis=0, concat_axis=0, tiled=True)  17.4 us
  transfers between devices with their start and end apart: 9, of which 7 were waited for; matrix products, arithmetic and copies ran while one was open for 20% of the time, Pallas kernels for 0%

profile of v1, /device:TPU:1, one launch (start us, length us, event | category | flops | bytes accessed | tf_op | source)
XLA Modules:
  0.0 475.5 jit_solution(1924967933561532296)
XLA Ops:
  11.6 12.0 %all-to-all-start = ((s32[32,32,1]{1,2,0:T(1,128)}), s32[32,32,1]{1,2,0:T(1,128)S(1)}, u32[]{:S(2)}, u32[]{:S(2)}) async-start(s32[32,32,1]{1,2,0:T(1,128)} %bitcast.2), calls=%async_computation | async-start | bytes 32768 | tf_op jit(solution)/shard_map/all_to_all | solution.py:79
  26.7 5.6 %all-to-all-done = s32[32,32,1]{1,2,0:T(1,128)S(1)} async-done(((s32[32,32,1]{1,2,0:T(1,128)}), s32[32,32,1]{1,2,0:T(1,128)S(1)}, u32[]{:S(2)}, u32[]{:S(2)}) %all-to-all-start) | async-done | bytes 4128 | tf_op jit(solution)/shard_map/all_to_all | solution.py:79
  32.3 3.9 all-to-all-start.4
  37.6 4.4 sort.35
  41.9 18.7 %all-to-all-done.4 = bf16[32,32,512]{2,1,0:T(8,128)(2,1)S(1)} async-done(((bf16[32,32,512]{2,1,0:T(8,128)(2,1)}), bf16[32,32,512]{2,1,0:T(8,128)(2,1)S(1)}, u32[]{:S(2)}, u32[]{:S(2)}) %all-to-all-start.4) | async-done | bytes 1048608 | tf_op jit(solution)/shard_map/all_to_all | solution.py:78
  67.2 54.9 %all_to_all.50 = bf16[32,32,1024]{2,1,0:T(8,128)(2,1)S(1)} all-to-all(bf16[32,32,1024]{2,1,0:T(8,128)(2,1)S(1)} %broadcast_select_fusion), channel_id=1, replica_groups=mesh['rep'=32,'tp'=8] {'rep'}, dimensions={0} | all-to-all | bytes 4194304 | tf_op jit(solution)/shard_map/all_to_all | solution.py:77
  128.1 8.2 %all-to-all-start.2 = ((bf16[32,256,128]{2,1,0:T(8,128)(2,1)}), bf16[32,256,128]{2,1,0:T(8,128)(2,1)S(1)}, u32[]{:S(2)}, u32[]{:S(2)}) async-start(bf16[32,256,128]{2,1,0:T(8,128)(2,1)} %stack.8), calls=%async_computation.2 | async-start | bytes 4194304 | tf_op jit(solution)/shard_map/all_to_all | solution.py:11
  139.3 3.9 fusion.2
  143.5 4.7 convolution_convert_fusion
  148.2 30.6 %all-gather.11.cloned.1.call-done = bf16[512,8192]{1,0:T(8,128)(2,1)} async-done(((bf16[512,1024]{1,0:T(8,128)(2,1)}), bf16[512,8192]{1,0:T(8,128)(2,1)}) %all-gather.11.cloned.1.call-update) | async-done | bytes 8388624 | tf_op jit(solution)/shard_map/all_gather | solution.py:84
  178.9 5.1 %fusion = f32[512]{0:T(512)S(1)} fusion(bf16[512,8192]{1,0:T(8,128)(2,1)} %all-gather.11.cloned.1.call-done), kind=kLoop, calls=%fused_computation.12 | loop fusion | flops 12582400 | bytes 8390656 | tf_op jit(solution)/shard_map/reduce_sum | solution.py:16
  184.0 95.4 %all-gather.9.cloned.1.call-done = bf16[8192,512]{1,0:T(8,128)(2,1)} async-done(((bf16[256,512]{1,0:T(8,128)(2,1)}), bf16[8192,512]{1,0:T(8,128)(2,1)}) %all-gather.9.cloned.1.call-update) | async-done | bytes 8388624 | tf_op jit(solution)/shard_map/all_gather | solution.py:96
  279.4 11.2 %convolution_convert_fusion.1 = bf16[512,512]{0,1:T(8,128)(2,1)} fusion(bf16[8192,512]{1,0:T(8,128)(2,1)} %all-gather.9.cloned.1.call-done, bf16[512,8192]{1,0:T(8,128)(2,1)} %all-gather.11.cloned.1.call-done, f32[512]{0:T(512)S(1)} %add_rsqrt_fusion.1), kind=kOutput, calls=%fused_computation.38 | convolution fusion | flops 4307812352 | bytes 17303552 | tf_op jit(solution)/shard_map/dot_general | solution.py:102
  290.6 62.8 %all-gather.7.cloned.1.call-done = bf16[8192,128]{1,0:T(8,128)(2,1)} async-done(((bf16[256,128]{1,0:T(8,128)(2,1)}), bf16[8192,128]{1,0:T(8,128)(2,1)}) %all-gather.7.cloned.1.call-update) | async-done | bytes 2097168 | tf_op jit(solution)/shard_map/all_gather | solution.py:97
  353.4 10.2 %fusion.4 = (f32[4,512]{1,0:T(4,128)S(1)}, f32[512,512,4]{1,0,2:T(8,128)}) fusion(pred[512,512]{0,1:T(8,128)(4,1)S(1)} %fusion.26, bf16[512,4,128]{0,2,1:T(8,128)(2,1)} %bitcast.122, bf16[8192,128]{1,0:T(8,128)(2,1)} %all-gather.7.cloned.1.call-done, bf16[512,8192]{1,0:T(8,128)(2,1)} %all-gather.11.cloned.1.call-done, f32[512]{0:T(512)S(1)} %add_rsqrt_fusion.1), kind=kOutput, calls=%fused_computation.24 | convolution fusion | flops 1357969408 | bytes 15476736 | tf_op jit(solution)/shard_map/pgjd,qgd->gjpq/dot_general | solution.py:27
  363.6 9.5 %fusion.6 = (f32[4,512]{1,0:T(4,128)S(1)}, f32[4,512]{1,0:T(4,128)S(1)}, f32[512,512,4]{1,0,2:T(8,128)}) fusion(f32[512,512,4]{1,0,2:T(8,128)} %get-tuple-element.14, f32[4,512]{1,0:T(4,128)S(1)} %get-tuple-element.13, pred[512,512]{0,1:T(8,128)(4,1)S(1)} %fusion.26, bf16[512,4,128]{0,2,1:T(8,128)(2,1)S(1)} %bitcast.121, bf16[4096,128]{1,0:T(8,128)(2,1)} %param.22, ...), kind=kOutput, calls=%fused_computation.26 | convolution fusion | flops 820047872 | bytes 14444544 | tf_op jit(solution)/shard_map/pgjd,qgd->gjpq/dot_general | solution.py:27
  376.3 6.6 %fusion.17 = bf16[128,4,512]{2,0,1:T(8,128)(2,1)S(1)} fusion(f32[4,512]{1,0:T(4,128)S(1)} %fusion.7, f32[4,512]{1,0:T(4,128)S(1)} %get-tuple-element.8, f32[512,512,4]{1,0,2:T(8,128)} %get-tuple-element.15, pred[512,512]{0,1:T(8,128)(4,1)S(1)} %fusion.26, bf16[4096,128]{1,0:T(8,128)(2,1)} %param.23, bf16[512,4096]{1,0:T(8,128)(2,1)} %all-gather.13.cloned.1.call-done, ...), kind=kOutput, calls=%fused_computation.37 | convolution fusion | flops 818216960 | bytes 10242048 | tf_op jit(solution)/shard_map/gjpq,qgd->pgjd/dot_general | solution.py:36
  388.0 5.3 %all-to-all-start.5 = ((bf16[32,32,512]{2,1,0:T(8,128)(2,1)}), bf16[32,32,512]{2,1,0:T(8,128)(2,1)S(1)}, u32[]{:S(2)}, u32[]{:S(2)}) async-start(bf16[32,32,512]{2,1,0:T(8,128)(2,1)} %bitcast.29), calls=%async_computation.5 | async-start | bytes 2097152 | tf_op jit(solution)/shard_map/all_to_all | solution.py:115
  393.2 9.1 %fusion.14 = bf16[128,4,512]{2,0,1:T(8,128)(2,1)S(1)} fusion(f32[4,512]{1,0:T(4,128)S(1)} %get-tuple-element.7, f32[4,512]{1,0:T(4,128)S(1)} %get-tuple-element.13, f32[512,512,4]{1,0,2:T(8,128)} %get-tuple-element.14, pred[512,512]{0,1:T(8,128)(4,1)S(1)} %fusion.26, bf16[8192,128]{1,0:T(8,128)(2,1)} %bitcast.114, ...), kind=kOutput, calls=%fused_computation.36 | convolution fusion | flops 1361379328 | bytes 15484928 | tf_op jit(solution)/shard_map/gjpq,qgd->pgjd/dot_general | solution.py:36
  402.7 3.5 scatter_custom_fusion
  406.1 6.4 %all-to-all-done.5 = bf16[32,32,512]{2,1,0:T(8,128)(2,1)S(1)} async-done(((bf16[32,32,512]{2,1,0:T(8,128)(2,1)}), bf16[32,32,512]{2,1,0:T(8,128)(2,1)S(1)}, u32[]{:S(2)}, u32[]{:S(2)}) %all-to-all-start.5) | async-done | bytes 1048608 | tf_op jit(solution)/shard_map/all_to_all | solution.py:115
  412.5 9.5 %all-to-all-start.3 = ((bf16[32,32,512]{2,1,0:T(8,128)(2,1)}), bf16[32,32,512]{2,1,0:T(8,128)(2,1)}, u32[]{:S(2)}, u32[]{:S(2)}) async-start(bf16[32,32,512]{2,1,0:T(8,128)(2,1)} %bitcast.15), calls=%async_computation.3 | async-start | bytes 2097152 | tf_op jit(solution)/shard_map/all_to_all | solution.py:114
  424.2 17.4 %all-to-all-done.3 = bf16[32,32,512]{2,1,0:T(8,128)(2,1)} async-done(((bf16[32,32,512]{2,1,0:T(8,128)(2,1)}), bf16[32,32,512]{2,1,0:T(8,128)(2,1)}, u32[]{:S(2)}, u32[]{:S(2)}) %all-to-all-start.3) | async-done | bytes 1048608 | tf_op jit(solution)/shard_map/all_to_all | solution.py:114
  446.7 21.4 %psum.7 = f32[2,1024]{1,0:T(2,128)S(1)} all-reduce(f32[2,1024]{1,0:T(2,128)S(1)} %pad_maximum_fusion), channel_id=1, replica_groups=mesh['rep'=32,'tp'=8] {'tp'}, use_global_device_ids=true, to_apply=%region_10.12 | all-reduce | flops 2048 | bytes 16384 | tf_op jit(solution)/shard_map/psum | solution.py:129
  (74 shorter events, 40.7 us)
Async XLA Ops:
  7.2 56.2 %copy-start = (bf16[1024,1024]{1,0:T(8,128)(2,1)S(1)}, bf16[1024,1024]{1,0:T(8,128)(2,1)}, u32[]{:S(2)}) copy-start(bf16[1024,1024]{1,0:T(8,128)(2,1)} %param.14) | copy-start | bytes 6291460
  11.6 20.7 %all-to-all-start = ((s32[32,32,1]{1,2,0:T(1,128)}), s32[32,32,1]{1,2,0:T(1,128)S(1)}, u32[]{:S(2)}, u32[]{:S(2)}) async-start(s32[32,32,1]{1,2,0:T(1,128)} %bitcast.2), calls=%async_computation | async-start | bytes 32768 | tf_op jit(solution)/shard_map/all_to_all | solution.py:79
  32.3 28.3 %all-to-all-start.4 = ((bf16[32,32,512]{2,1,0:T(8,128)(2,1)}), bf16[32,32,512]{2,1,0:T(8,128)(2,1)S(1)}, u32[]{:S(2)}, u32[]{:S(2)}) async-start(bf16[32,32,512]{2,1,0:T(8,128)(2,1)} %broadcast_select_fusion.1), calls=%async_computation.4 | async-start | bytes 2097152 | tf_op jit(solution)/shard_map/all_to_all | solution.py:78
  36.2 103.1 %all-gather.13.cloned.1.call-start = ((), (), s32[]{:S(2)}) async-start(), calls=%async_computation.9 | async-start | bytes 4718592 | tf_op jit(solution)/shard_map/all_gather | solution.py:85
  63.3 115.6 %all-gather.11.cloned.1.call-start = ((), (), s32[]{:S(2)}) async-start(), calls=%async_computation.8 | async-start | bytes 9437184 | tf_op jit(solution)/shard_map/all_gather | solution.py:84
  122.2 4.2 copy-start.5
  125.0 154.4 %all-gather.9.cloned.1.call-start = ((), (), s32[]{:S(2)}) async-start(), calls=%async_computation.7 | async-start | bytes 8650752 | tf_op jit(solution)/shard_map/all_gather | solution.py:96
  125.8 227.6 %all-gather.7.cloned.1.call-start = ((), (), s32[]{:S(2)}) async-start(), calls=%async_computation.6 | async-start | bytes 2162688 | tf_op jit(solution)/shard_map/all_gather | solution.py:97
  128.1 258.5 %all-to-all-start.2 = ((bf16[32,256,128]{2,1,0:T(8,128)(2,1)}), bf16[32,256,128]{2,1,0:T(8,128)(2,1)S(1)}, u32[]{:S(2)}, u32[]{:S(2)}) async-start(bf16[32,256,128]{2,1,0:T(8,128)(2,1)} %stack.8), calls=%async_computation.2 | async-start | bytes 4194304 | tf_op jit(solution)/shard_map/all_to_all | solution.py:11
  139.3 4.2 copy-start.3
  386.6 1.4 copy-start.4
  388.0 24.5 %all-to-all-start.5 = ((bf16[32,32,512]{2,1,0:T(8,128)(2,1)}), bf16[32,32,512]{2,1,0:T(8,128)(2,1)S(1)}, u32[]{:S(2)}, u32[]{:S(2)}) async-start(bf16[32,32,512]{2,1,0:T(8,128)(2,1)} %bitcast.29), calls=%async_computation.5 | async-start | bytes 2097152 | tf_op jit(solution)/shard_map/all_to_all | solution.py:115
  402.4 19.6 %copy-start.7 = (bf16[512]{0:T(512)(128)(2,1)S(1)}, bf16[512]{0:T(512)(128)(2,1)}, u32[]{:S(2)}) copy-start(bf16[512]{0:T(512)(128)(2,1)} %param.24) | copy-start | bytes 3076
  402.4 19.6 %copy-start.8 = (bf16[512]{0:T(512)(128)(2,1)S(1)}, bf16[512]{0:T(512)(128)(2,1)}, u32[]{:S(2)}) copy-start(bf16[512]{0:T(512)(128)(2,1)} %param.25) | copy-start | bytes 3076
  402.4 19.7 %copy-start.9 = (s32[1,32]{1,0:T(1,128)S(1)}, s32[1,32]{1,0:T(1,128)}, u32[]{:S(2)}) copy-start(s32[1,32]{1,0:T(1,128)} %param.17) | copy-start | bytes 388
  402.4 19.7 %copy-start.6 = (s32[1024]{0:T(1024)S(1)}, s32[1024]{0:T(1024)}, u32[]{:S(2)}) copy-start(s32[1024]{0:T(1024)} %param.16) | copy-start | bytes 12292
  412.5 9.6 %copy-start.2 = (bf16[32,32,512]{2,1,0:T(8,128)(2,1)}, bf16[32,32,512]{2,1,0:T(8,128)(2,1)S(1)}, u32[]{:S(2)}) copy-start(bf16[32,32,512]{2,1,0:T(8,128)(2,1)S(1)} %all-to-all-done.5) | copy-start | bytes 3145732
  412.5 29.1 %all-to-all-start.3 = ((bf16[32,32,512]{2,1,0:T(8,128)(2,1)}), bf16[32,32,512]{2,1,0:T(8,128)(2,1)}, u32[]{:S(2)}, u32[]{:S(2)}) async-start(bf16[32,32,512]{2,1,0:T(8,128)(2,1)} %bitcast.15), calls=%async_computation.3 | async-start | bytes 2097152 | tf_op jit(solution)/shard_map/all_to_all | solution.py:114
  422.1 46.6 %copy-start.1 = (bf16[1024,1024]{1,0:T(8,128)(2,1)S(1)}, bf16[1024,1024]{1,0:T(8,128)(2,1)}, u32[]{:S(2)}) copy-start(bf16[1024,1024]{1,0:T(8,128)(2,1)} %param.14) | copy-start | bytes 6291460
Sparse Core Ops, SparseCore 0:
  63.4 36.1 all-gather.12
  125.1 53.6 all-gather.10
  181.5 97.8 all-gather.8
  281.8 71.5 all-gather.6
